TPU v7x, 128 devices: a whole 4x4x4 slice. The times are simulated.
128 devices in a mesh: wide: 16 (over z_lo, x, core), node: 8 (over y, z_hi).
Axes of the slice: x: 4, y: 4, z: 4 (z_hi: 2, z_lo: 2; z = z_hi * 2 + z_lo), core: 2. Of those that a mesh axis runs over, the one named last changes fastest.
Arguments:
- normed: bfloat16 [65536, 4096], P(('wide', 'node')), may hold values from -24 to 24
- queries: bfloat16 [65536, 2048], P(('wide', 'node')), may hold values from -48 to 48
- keys: bfloat16 [65536, 512], P(('wide', 'node')), may hold values from -6 to 6
- values: bfloat16 [65536, 512], P(('wide', 'node')), may hold values from -6 to 6
- attn_grad: bfloat16 [65536, 2048], P(('wide', 'node')), may hold values from -6 to 6
- kv_proj: bfloat16 [4096, 1024], P(None, 'node'), may hold values from -0.09375 to 0.09375
Outputs:
- query_grad: bfloat16 [65536, 2048], P(('wide', 'node'))
- input_grad: bfloat16 [65536, 4096], P(('wide', 'node'))
- weight_grad: float32 [4096, 1024], P(('wide', 'node'))
All inputs are finite; a program needn't handle non-finite values.
Results may differ from a plain program's by a relative error of at most 0.019.
Values may be sent and summed in bfloat16 or wider, within the bound.
No kernel may reach another device: no remote copies, remote signals or barrier semaphores. Data moves between devices by JAX's collectives and lax.ppermute only.
A program may use at most 192 MiB of HBM per device.

v0:
```python
import jax
import jax.numpy as jnp
from jax import lax
from jax.sharding import PartitionSpec as P

HQ = 16
KVH = 4
HD = 128


ROPE_BASE = 500000.0


def split_up(shard, dim, count):
    lengths = shard.shape
    parts = shard.reshape(*lengths[:dim], count, lengths[dim] // count, *lengths[dim + 1 :])
    return jnp.moveaxis(parts, dim, 0)


def summed_on_arrival(shard, axis, dim):
    parts = split_up(shard, dim, lax.axis_size(axis))
    arrived = lax.all_to_all(parts, axis, split_axis=0, concat_axis=0, tiled=True)
    return arrived.astype(jnp.float32).sum(axis=0)


def rope_tables(length, size):
    half_size = size // 2
    frequency = jnp.power(
        jnp.float32(ROPE_BASE), -jnp.arange(half_size, dtype=jnp.float32) * (2.0 / size)
    )
    angles = jnp.arange(length, dtype=jnp.float32)[:, None] * frequency[None, :]
    cosine = jnp.concatenate([jnp.cos(angles), jnp.cos(angles)], axis=1)
    sine_tab = jnp.concatenate([jnp.sin(angles), jnp.sin(angles)], axis=1)
    return (cosine, sine_tab)


def sequence_grads(queries, keys, values, attn_grad, cosine, sine_tab):
    length = queries.shape[0]
    query_heads = queries.reshape(length, KVH, HQ // KVH, HD)
    key_heads = keys.reshape(length, KVH, HD)
    value_heads = values.reshape(length, KVH, HD)
    grad_heads = attn_grad.reshape(length, KVH, HQ // KVH, HD)
    inv_root = HD ** (-0.5)
    scores = (
        jnp.einsum("tkgd,skd->kgts", query_heads, key_heads, preferred_element_type=jnp.float32)
        * inv_root
    )
    positions = jnp.arange(length, dtype=jnp.int32)
    causal_mask = positions[:, None] >= positions[None, :]
    scores = jnp.where(causal_mask, scores, -jnp.inf)
    row_max = jnp.max(scores, axis=-1, keepdims=True)
    exponent = jnp.exp(scores - row_max)
    prob_full = exponent / jnp.sum(exponent, axis=-1, keepdims=True)
    prob_low = prob_full.astype(jnp.bfloat16)
    grad_prob = jnp.einsum(
        "tkgd,skd->kgts", grad_heads, value_heads, preferred_element_type=jnp.float32
    )
    row_delta = jnp.sum(prob_full * grad_prob, axis=-1, keepdims=True)
    grad_score = (prob_full * (grad_prob - row_delta) * inv_root).astype(jnp.bfloat16)
    query_grad = jnp.einsum(
        "kgts,skd->tkgd", grad_score, key_heads, preferred_element_type=jnp.float32
    )
    query_grad = query_grad.astype(jnp.bfloat16).reshape(length, HQ * HD)
    key_grad = jnp.einsum(
        "kgts,tkgd->skd", grad_score, query_heads, preferred_element_type=jnp.float32
    )
    value_grad = jnp.einsum(
        "kgts,tkgd->skd", prob_low, grad_heads, preferred_element_type=jnp.float32
    ).astype(jnp.bfloat16)
    half_size = HD // 2
    sine_part = key_grad * sine_tab[:, None, :]
    key_unrot = key_grad * cosine[:, None, :] + jnp.concatenate(
        [sine_part[..., half_size:], -sine_part[..., :half_size]], axis=-1
    )
    kv_grad = jnp.concatenate(
        [
            key_unrot.astype(jnp.bfloat16).reshape(length, KVH * HD),
            value_grad.reshape(length, KVH * HD),
        ],
        axis=1,
    )
    return (query_grad, kv_grad)


def local(normed, queries, keys, values, attn_grad, kv_proj):
    length = normed.shape[0]
    cosine, sine_tab = rope_tables(length, HD)
    query_grad, kv_grad = sequence_grads(queries, keys, values, attn_grad, cosine, sine_tab)
    summed = lax.dot_general(
        kv_grad,
        lax.all_gather(kv_proj, "node", axis=1, tiled=True),
        (((1,), (1,)), ((), ())),
        preferred_element_type=jnp.float32,
    )
    input_grad = summed.astype(jnp.bfloat16)
    wide_count = lax.axis_size("wide")
    node_count = lax.axis_size("node")
    grad_scale = (length * wide_count * node_count) ** (-0.5)
    local_term = (
        lax.dot_general(
            normed, kv_grad, (((0,), (0,)), ((), ())), preferred_element_type=jnp.float32
        )
        * grad_scale
    )
    partial_value = lax.psum_scatter(
        local_term.astype(jnp.bfloat16), "wide", scatter_dimension=0, tiled=True
    )
    weight_grad = summed_on_arrival(partial_value, "node", 0)
    return (query_grad, input_grad, weight_grad)


def solution(mesh):
    return jax.shard_map(
        local,
        mesh=mesh,
        in_specs=(
            P(("wide", "node"), None),
            P(("wide", "node"), None),
            P(("wide", "node"), None),
            P(("wide", "node"), None),
            P(("wide", "node"), None),
            P(None, "node"),
        ),
        out_specs=(P(("wide", "node"), None), P(("wide", "node"), None), P(("wide", "node"), None)),
        check_vma=False,
    )
```

profile of v0, /device:TPU:6, one launch (start us, length us, event | category | flops | bytes accessed | tf_op | source)
XLA Modules:
  0.0 258.2 jit_solution(9317484097268923154)
XLA Ops:
  8.0 0.0 reduce-scatter.2.cloned.1.call-start
  8.1 0.8 iota_compare_fusion
  8.8 0.5 fusion.29
  9.4 1.2 reshape.41
  10.6 0.3 copy.35
  10.9 1.2 reshape.43
  12.0 3.9 %copy.46 = bf16[512,2048]{0,1:T(8,128)(2,1)} copy(bf16[512,2048]{1,0:T(8,128)(2,1)} %param.7) | data formatting | bytes 4194304 | tf_op jit(solution)/shard_map/reshape | solution.py:39
  16.0 2.9 %copy.47 = bf16[512,2048]{0,1:T(8,128)(2,1)S(1)} copy(bf16[512,2048]{1,0:T(8,128)(2,1)} %param.10) | data formatting | bytes 4194304 | tf_op jit(solution)/shard_map/reshape | solution.py:42
  18.8 8.0 %fusion.26 = f32[4,512,512,4]{2,1,3,0:T(8,128)} fusion(bf16[512,4,4,128]{0,3,2,1:T(8,128)(2,1)S(1)} %bitcast.76, bf16[512,4,128,1]{2,1,0,3:T(4,128)(2,1)S(1)} %bitcast.78), kind=kOutput, calls=%fused_computation.34 | convolution fusion | flops 1073741824 | bytes 19398656 | tf_op jit(solution)/shard_map/tkgd,skd->kgts/dot_general | solution.py:55
  26.9 10.2 %fusion.39 = (f32[4,4,512]{2,1,0:T(4,128)S(1)}, f32[4,4,512,512]{2,3,1,0:T(8,128)}) fusion(pred[512,512]{0,1:T(8,128)(4,1)} %iota_compare_fusion, bf16[512,4,128,1]{0,2,3,1:T(8,128)(2,1)S(1)} %copy.35, bf16[512,4,4,128]{0,3,2,1:T(8,128)(2,1)} %bitcast.79), kind=kOutput, calls=%fused_computation.51 | convolution fusion | flops 1090519552 | bytes 19693568 | tf_op jit(solution)/shard_map/sub | solution.py:52
  37.1 9.4 %fusion.22 = bf16[4,512,128]{1,2,0:T(8,128)(2,1)} fusion(bf16[512,4,4,128]{0,3,2,1:T(8,128)(2,1)S(1)} %bitcast.77, f32[4,4,512,512]{2,3,1,0:T(8,128)} %get-tuple-element.14, f32[4,4,512]{2,1,0:T(4,128)S(1)} %get-tuple-element.13), kind=kOutput, calls=%fused_computation.26 | convolution fusion | flops 1082392576 | bytes 19431424 | tf_op jit(solution)/shard_map/kgts,tkgd->skd/dot_general | solution.py:67
  46.5 0.0 copy-start
  46.5 27.0 %fusion.18 = f32[4,512,128]{1,2,0:T(8,128)S(1)} fusion(bf16[512,4,4,128]{0,3,2,1:T(8,128)(2,1)} %bitcast.80, f32[4,512,512,4]{2,1,3,0:T(8,128)} %fusion.26, f32[4,4,512,512]{2,3,1,0:T(8,128)} %get-tuple-element.14, f32[4,4,512]{2,1,0:T(4,128)S(1)} %get-tuple-element.13), kind=kOutput, calls=%fused_computation.24 | convolution fusion | flops 1103110656 | bytes 36732928 | tf_op jit(solution)/shard_map/kgts,tkgd->skd/dot_general | solution.py:64
  73.5 0.1 multiply_bitcast_fusion
  73.7 0.1 fusion.38
  73.8 0.3 fusion.25
  74.1 0.0 copy-done
  74.1 9.6 %fusion.14 = bf16[4096,1024]{0,1:T(8,128)(2,1)} fusion(bf16[512,4096]{1,0:T(8,128)(2,1)} %param.6, bf16[512,512]{0,1:T(8,128)(2,1)S(1)} %bitcast.86, bf16[512,512]{0,1:T(8,128)(2,1)S(1)} %bitcast.83), kind=kOutput, calls=%fused_computation.20 | convolution fusion | flops 4305453056 | bytes 13631488 | tf_op jit(solution)/shard_map/dot_general | solution.py:100
  83.7 0.0 reduce-scatter.2.cloned.1.call-update
  83.7 0.0 all-gather.2.cloned.1.call-start
  83.8 0.5 all-gather.2.cloned.1.call-update
  84.3 27.4 %fusion.15 = bf16[4,4,512,128]{2,3,1,0:T(8,128)(2,1)S(1)} fusion(bf16[512,4,128,1]{0,2,3,1:T(8,128)(2,1)S(1)} %copy.35, f32[4,512,512,4]{2,1,3,0:T(8,128)} %fusion.26, f32[4,4,512,512]{2,3,1,0:T(8,128)} %get-tuple-element.14, f32[4,4,512]{2,1,0:T(4,128)S(1)} %get-tuple-element.13), kind=kOutput, calls=%fused_computation.22 | convolution fusion | flops 1104159232 | bytes 36208640 | tf_op jit(solution)/shard_map/kgts,skd->tkgd/dot_general | solution.py:60
  111.7 2.4 copy.31
  114.1 44.0 %reduce-scatter.2.cloned.1.call-done = bf16[256,1024]{0,1:T(8,128)(2,1)} async-done(((bf16[4096,1024]{0,1:T(8,128)(2,1)}), bf16[256,1024]{0,1:T(8,128)(2,1)}) %reduce-scatter.2.cloned.1.call-update) | async-done | bytes 524304 | tf_op jit(solution)/shard_map/reduce_scatter | solution.py:105
  158.1 2.1 copy.30
  160.2 6.1 %all-to-all-start = ((bf16[8,32,1024]{2,1,0:T(8,128)(2,1)}), bf16[8,32,1024]{2,1,0:T(8,128)(2,1)S(1)}, u32[]{:S(2)}, u32[]{:S(2)}) async-start(bf16[8,32,1024]{2,1,0:T(8,128)(2,1)} %bitcast.17), calls=%async_computation.1 | async-start | bytes 1048576 | tf_op jit(solution)/shard_map/all_to_all | solution.py:22
  166.3 73.6 %all-gather.2.cloned.1.call-done = bf16[4096,1024]{1,0:T(8,128)(2,1)} async-done(((bf16[4096,128]{1,0:T(8,128)(2,1)}), bf16[4096,1024]{1,0:T(8,128)(2,1)}) %all-gather.2.cloned.1.call-update) | async-done | bytes 8388624 | tf_op jit(solution)/shard_map/all_gather | solution.py:91
  239.9 10.1 %convolution_convert_fusion = bf16[512,4096]{1,0:T(8,128)(2,1)} fusion(bf16[4096,1024]{1,0:T(8,128)(2,1)} %all-gather.2.cloned.1.call-done, bf16[512,512]{0,1:T(8,128)(2,1)} %bitcast.85, bf16[512,512]{0,1:T(8,128)(2,1)S(1)} %bitcast.84), kind=kOutput, calls=%fused_computation.21 | convolution fusion | flops 4299161600 | bytes 13631488 | tf_op jit(solution)/shard_map/dot_general | solution.py:89
  250.1 0.0 all-to-all-done
  250.1 0.7 convert_reduce_fusion
  (2 shorter events, 0.0 us)
Async XLA Ops:
  8.0 150.2 %reduce-scatter.2.cloned.1.call-start = ((), (), s32[]{:S(2)}) async-start(), calls=%async_computation.3 | async-start | bytes 8912896 | tf_op jit(solution)/shard_map/reduce_scatter | solution.py:105
  46.5 27.6 %copy-start = (bf16[4,512,128]{1,2,0:T(8,128)(2,1)S(1)}, bf16[4,512,128]{1,2,0:T(8,128)(2,1)}, u32[]{:S(2)}) copy-start(bf16[4,512,128]{1,2,0:T(8,128)(2,1)} %fusion.22) | copy-start | bytes 1572868
  83.7 156.2 %all-gather.2.cloned.1.call-start = ((), (), s32[]{:S(2)}) async-start(), calls=%async_computation.2 | async-start | bytes 9437184 | tf_op jit(solution)/shard_map/all_gather | solution.py:91
  160.2 89.8 %all-to-all-start = ((bf16[8,32,1024]{2,1,0:T(8,128)(2,1)}), bf16[8,32,1024]{2,1,0:T(8,128)(2,1)S(1)}, u32[]{:S(2)}, u32[]{:S(2)}) async-start(bf16[8,32,1024]{2,1,0:T(8,128)(2,1)} %bitcast.17), calls=%async_computation.1 | async-start | bytes 1048576 | tf_op jit(solution)/shard_map/all_to_all | solution.py:22
Sparse Core Ops, SparseCore 0:
  83.8 74.2 reduce-scatter.1
Sparse Core Ops, SparseCore 1:
  86.4 153.5 all-gather.1
where the time goes:
time: 259 us; the launch traced here: 258 us
  waiting for transfers between devices  118 us (46%)
  matrix products  102 us (39%)
  between operations  15.6 us (6%)
  local copies, waits for them, and re-layouts  13.9 us (5%)
  starting transfers between devices  6.21 us (2%)
  other arithmetic  2.62 us (1%)
    all_gather x1, waiting for transfers between devices, local(): lax.all_gather(kv_proj, 'node', axis=1, tiled=True)  73.6 us
    reduce_scatter x1, waiting for transfers between devices, local(): lax.psum_scatter(local_term.astype(jnp.bfloat16), 'wide', scatter_dimensi...  44 us
    dot_general x1, matrix products, sequence_grads(): jnp.einsum('kgts,skd->tkgd', grad_score, key_heads, preferred_element_typ...  27.4 us
    dot_general x1, matrix products, sequence_grads(): jnp.einsum('kgts,tkgd->skd', grad_score, query_heads, preferred_element_t...  27 us
    sub x1, matrix products, sequence_grads(): exponent = jnp.exp(scores - row_max)  10.2 us
    dot_general x1, matrix products, local(): lax.dot_general(kv_grad, lax.all_gather(kv_proj, 'node', axis=1, tiled=Tr...  10.1 us
    dot_general x1, matrix products, local(): lax.dot_general(normed, kv_grad, (((0,), (0,)), ((), ())), preferred_elem...  9.6 us
    dot_general x1, matrix products, sequence_grads(): jnp.einsum('kgts,tkgd->skd', prob_low, grad_heads, preferred_element_type...  9.42 us
  transfers between devices with their start and end apart: 3, of which 2 were waited for; matrix products, arithmetic and copies ran while one was open for 16% of the time, Pallas kernels for 0%

commit v1 on v0

v1 whole, which is shorter than its diff:
```python
import functools

import jax
import jax.numpy as jnp
import numpy as np
from jax import lax
from jax.experimental import pallas as pl
from jax.experimental.pallas import tpu as pltpu
from jax.sharding import Mesh
from jax.sharding import PartitionSpec as P


KVH = 4
HD = 128
GROUP = 4
ROPE_BASE = 500000.0
LOG2E = 1.4426950408889634
INPUT_TILE = 1024
ATTENTION_VMEM = 60 << 20
WEIGHT_VMEM = 60 << 20
INPUT_VMEM = 24 << 20
AXES = ("zl", "x", "c", "y", "zh")
F32 = jnp.float32
BF = jnp.bfloat16


def permutation(move):
    pairs = []
    for zl in range(2):
        for x in range(4):
            for c in range(2):
                for y in range(4):
                    for zh in range(2):
                        source = ((zl * 4 + x) * 2 + c) * 8 + y * 2 + zh
                        tx, tc, ty, tz = move(x, c, y, zh * 2 + zl)
                        pairs.append((source, (((tz % 2) * 4 + tx) * 2 + tc) * 8 + ty * 2 + tz // 2))
    return pairs


PARTNER = permutation(lambda x, c, y, z: (x, 1 - c, y, z))
Z_HALF = permutation(lambda x, c, y, z: (x, c, y, z ^ 2))
ALONG_Y = {k: permutation(lambda x, c, y, z: (x, c, y ^ k, z)) for k in (1, 2, 3)}
FIRST = {
    k: permutation(lambda x, c, y, z: (x ^ k, c, y, z) if c == 0 else (x, c, y, z ^ k))
    for k in (1, 2, 3)
}
SECOND = {
    k: permutation(lambda x, c, y, z: (x, c, y, z ^ k) if c == 0 else (x ^ k, c, y, z))
    for k in (1, 2, 3)
}


def rope_tables(length, size):
    half_size = size // 2
    frequency = ROPE_BASE ** (-np.arange(half_size) * (2.0 / size))
    angles = np.arange(length)[:, None] * frequency[None, :]
    return jnp.asarray(np.cos(angles), F32), jnp.asarray(np.sin(angles), F32)


def dot(a, b, da, db):
    return lax.dot_general(a, b, (((da,), (db,)), ((), ())), preferred_element_type=F32)


def attention_kernel(
    q_any, k_any, v_any, do_any, cos_any, sin_any, dq_any, kv_any, away_any, *scratch, block
):
    q_all, k_all, v_all, do_all, cos_ref, sin_ref, dq_all, kv_all, dk_acc, dv_acc = scratch[:10]
    in_sems, table_sems, out_sems = scratch[10:]
    length = q_all.shape[1]
    width = GROUP * HD
    inv_root = HD ** (-0.5)
    blocks = length // block
    first = lax.axis_index("c") == 0

    def loads(g):
        wide = pl.ds(pl.multiple_of(g * width, width), width)
        narrow = pl.ds(pl.multiple_of(g * HD, HD), HD)
        return [
            pltpu.make_async_copy(k_any.at[:, narrow], k_all.at[g], in_sems.at[g, 0]),
            pltpu.make_async_copy(q_any.at[:, wide], q_all.at[g], in_sems.at[g, 1]),
            pltpu.make_async_copy(v_any.at[:, narrow], v_all.at[g], in_sems.at[g, 2]),
            pltpu.make_async_copy(do_any.at[:, wide], do_all.at[g], in_sems.at[g, 3]),
        ]

    def stores(g):
        wide = pl.ds(pl.multiple_of(g * width, width), width)
        narrow = pl.ds(pl.multiple_of(g * HD, HD), HD)
        return [
            pltpu.make_async_copy(dq_all.at[g], dq_any.at[:, wide], out_sems.at[g, 0]),
            pltpu.make_async_copy(kv_all.at[g], kv_any.at[:, :, narrow], out_sems.at[g, 1]),
            pltpu.make_async_copy(kv_all.at[g, 1], away_any.at[:, narrow], out_sems.at[g, 2]),
        ]

    tables = [
        pltpu.make_async_copy(cos_any, cos_ref, table_sems.at[0]),
        pltpu.make_async_copy(sin_any, sin_ref, table_sems.at[1]),
    ]
    for load in loads(0) + loads(1) + tables + loads(2) + loads(3):
        load.start()
    rows = lax.broadcasted_iota(jnp.int32, (block, GROUP * block), 0)
    cols = lax.broadcasted_iota(jnp.int32, (block, GROUP * block), 1)
    keep = rows <= lax.rem(cols, block)

    def group(g, _):
        for load in loads(g):
            load.wait()
        k = k_all[g]
        v = v_all[g]
        for b in reversed(range(blocks)):
            end = (b + 1) * block
            part = slice(b * block, end)
            queries = jnp.concatenate(
                [q_all[g, part, j * HD : (j + 1) * HD] for j in range(GROUP)], axis=0
            )
            grads = jnp.concatenate(
                [do_all[g, part, j * HD : (j + 1) * HD] for j in range(GROUP)], axis=0
            )
            scores = dot(k[:end], queries, 1, 1)
            grad_prob = dot(v[:end], grads, 1, 1)
            diagonal = jnp.where(keep, scores[end - block :], -jnp.inf)
            if b:
                scores = jnp.concatenate([scores[: end - block], diagonal], axis=0)
            else:
                scores = diagonal
            top = jnp.max(scores, axis=0, keepdims=True)
            exponent = jnp.exp2((scores - top) * (LOG2E * inv_root))
            inv_sum = 1.0 / jnp.sum(exponent, axis=0, keepdims=True)
            delta = jnp.sum(exponent * grad_prob, axis=0, keepdims=True) * inv_sum
            prob_low = (exponent * inv_sum).astype(BF)
            grad_score = (exponent * (grad_prob - delta) * (inv_sum * inv_root)).astype(BF)
            dk = dot(grad_score, queries, 1, 0)
            dv = dot(prob_low, grads, 1, 0)
            if b == blocks - 1:
                dk_acc[...] = dk
                dv_acc[...] = dv
            else:
                dk_acc[:end, :] += dk
                dv_acc[:end, :] += dv
            dq = dot(grad_score, k[:end], 0, 0)
            for j in range(GROUP):
                dq_all[g, part, j * HD : (j + 1) * HD] = dq[j * block : (j + 1) * block].astype(BF)

        @pl.when(g == 0)
        def _():
            for load in tables:
                load.wait()

        key_grad = dk_acc[...]
        half = HD // 2
        cosine, sine = cos_ref[...], sin_ref[...]
        low, high = key_grad[:, :half], key_grad[:, half:]
        key_part = jnp.concatenate(
            [low * cosine + high * sine, high * cosine - low * sine], axis=1
        ).astype(BF)
        value_part = dv_acc[...].astype(BF)
        kv_all[g, 0] = jnp.where(first, key_part, value_part)
        kv_all[g, 1] = jnp.where(first, value_part, key_part)
        for store in stores(g):
            store.start()
        return 0

    lax.fori_loop(0, KVH, group, 0)
    for g in range(KVH):
        for store in stores(g):
            store.wait()


def attention(q, k, v, do, cosine, sine_tab):
    length = q.shape[0]
    width = GROUP * HD
    wide = pltpu.VMEM((KVH, length, width), BF)
    narrow = pltpu.VMEM((KVH, length, HD), BF)
    table = pltpu.VMEM((length, HD // 2), F32)
    total = pltpu.VMEM((length, HD), F32)
    return pl.pallas_call(
        functools.partial(attention_kernel, block=128),
        in_specs=[pl.BlockSpec(memory_space=pl.ANY)] * 6,
        out_specs=[pl.BlockSpec(memory_space=pl.ANY)] * 3,
        scratch_shapes=[
            wide,
            narrow,
            narrow,
            wide,
            table,
            table,
            wide,
            pltpu.VMEM((KVH, 2, length, HD), BF),
            total,
            total,
            pltpu.SemaphoreType.DMA((KVH, 4)),
            pltpu.SemaphoreType.DMA((2,)),
            pltpu.SemaphoreType.DMA((KVH, 3)),
        ],
        out_shape=[
            jax.ShapeDtypeStruct((length, KVH * width), BF),
            jax.ShapeDtypeStruct((2, length, KVH * HD), BF),
            jax.ShapeDtypeStruct((length, KVH * HD), BF),
        ],
        compiler_params=pltpu.CompilerParams(vmem_limit_bytes=ATTENTION_VMEM),
        name="attention",
    )(q, k, v, do, cosine, sine_tab)


def weight_kernel(
    own_ref, other_ref, kv_ref, kv_other_ref, *refs, scale, low
):
    outs, own, other, ka_ref, kb_ref, made, in_sems, kv_sems, out_sems = refs[:2], *refs[2:]
    zl, x, c, y, zh = (lax.axis_index(axis) for axis in AXES)
    cols = kb_ref.shape[1]
    width = own.shape[2]

    def source(e):
        along_x = (e // 2) * 4 + lax.bitwise_xor(x, low + 2 * (e % 2))
        along_z = lax.bitwise_xor(zl, low) * 4 + e
        start = jnp.where(c == 0, along_x, along_z) * width
        return pl.ds(pl.multiple_of(start, width), width)

    kv_load = pltpu.make_async_copy(kv_ref.at[0], ka_ref, kv_sems.at[0])
    kv_other_load = pltpu.make_async_copy(kv_other_ref, kb_ref, kv_sems.at[1])
    kv_load.start()
    loads = []
    for e in range(4):
        if e == 1:
            kv_other_load.start()
        for side, (ref, buffer) in enumerate(((own_ref, own), (other_ref, other))):
            load = pltpu.make_async_copy(ref.at[:, source(e)], buffer.at[e], in_sems.at[e, side])
            load.start()
            loads.append(load)
    for e in range(4):
        if e == 0:
            kv_load.wait()
        loads[2 * e].wait()
        value = dot(own[e], ka_ref[...], 0, 0)
        if e == 0:
            kv_other_load.wait()
        loads[2 * e + 1].wait()
        value += dot(other[e], kb_ref[...], 0, 0)
        value = (value * scale).astype(BF).reshape(2, 4, 2, 32, cols)
        to_zl = jnp.where(c == 0, e // 2, lax.bitwise_xor(zl, low))
        kx = jnp.where(c == 0, low + 2 * (e % 2), lax.bitwise_xor(e, x))
        for to_zh in range(2):
            kz = lax.bitwise_xor(to_zh, zh) * 2 + lax.bitwise_xor(to_zl, zl)
            first = jnp.where(c == 0, kx, kz) >> 1
            second = jnp.where(c == 0, kz, kx)
            for to_c in range(2):
                for to_y in range(4):
                    kc, ky = lax.bitwise_xor(to_c, c), lax.bitwise_xor(to_y, y)
                    made[first, second, ky, kc] = value[to_c, to_y, to_zh]
            for k in range(2):

                @pl.when(first == k)
                def _():
                    pltpu.make_async_copy(
                        made.at[k, second], outs[k].at[second], out_sems.at[k, second]
                    ).start()

    for k in range(2):
        for second in range(4):
            pltpu.make_async_copy(
                made.at[k, second], outs[k].at[second], out_sems.at[k, second]
            ).wait()


def weight_terms(own, other, kv, kv_other, scale, low):
    tokens, width = own.shape
    cols = kv.shape[2]
    shape = (4, 4, 2, 32, cols)
    anywhere = pl.BlockSpec(memory_space=pl.ANY)
    return pl.pallas_call(
        functools.partial(weight_kernel, scale=scale, low=low),
        in_specs=[anywhere] * 4,
        out_specs=[anywhere] * 2,
        scratch_shapes=[
            pltpu.VMEM((4, tokens, width // 8), BF),
            pltpu.VMEM((4, tokens, width // 8), BF),
            pltpu.VMEM((tokens, cols), BF),
            pltpu.VMEM((tokens, cols), BF),
            pltpu.VMEM((2,) + shape, BF),
            pltpu.SemaphoreType.DMA((4, 2)),
            pltpu.SemaphoreType.DMA((2,)),
            pltpu.SemaphoreType.DMA((2, 4)),
        ],
        out_shape=[jax.ShapeDtypeStruct(shape, BF) for _ in range(2)],
        compiler_params=pltpu.CompilerParams(vmem_limit_bytes=WEIGHT_VMEM),
        name="weight_terms",
    )(own, other, kv, kv_other)


def input_kernel(place, *refs):
    kvs, blocks, out_ref = refs[:8], refs[8:16], refs[-1]
    kv = jnp.concatenate([r[0] for r in kvs], axis=1)
    weights = jnp.concatenate([r[...] for r in blocks], axis=1)
    out_ref[...] = dot(kv, weights, 1, 1).astype(BF)


def input_grads(place, kv, own_proj, blocks, turn, earlier=None):
    length = kv.shape[1]
    depth = own_proj.shape[0]
    tile = INPUT_TILE
    half = depth // tile // 2

    def kv_map(j):
        k, h = j % 4, j // 4

        def index(i, p):
            node = lax.bitwise_xor(p[1], k) * 2 + lax.bitwise_xor(p[2], h)
            return (lax.bitwise_xor(node // 4, p[0]), 0, node & 3)

        return index

    def own_map(i, p):
        return (lax.bitwise_xor(p[0], turn) * half + i, 0)

    def out_map(i, p):
        return (0, lax.bitwise_xor(p[0], turn) * half + i)

    in_specs = [pl.BlockSpec((1, length, HD), kv_map(j)) for j in range(8)]
    in_specs += [pl.BlockSpec((tile, HD), own_map)]
    in_specs += [pl.BlockSpec((tile, HD), lambda i, p: (i, 0)) for _ in range(7)]
    operands = [place, *([kv] * 8), own_proj, *blocks]
    aliases = {}
    if earlier is not None:
        in_specs += [pl.BlockSpec(memory_space=pl.ANY)]
        aliases = {len(operands): 0}
        operands += [earlier]
    return pl.pallas_call(
        input_kernel,
        grid_spec=pltpu.PrefetchScalarGridSpec(
            num_scalar_prefetch=1,
            grid=(half,),
            in_specs=in_specs,
            out_specs=pl.BlockSpec((length, tile), out_map),
        ),
        out_shape=jax.ShapeDtypeStruct((length, depth), BF),
        input_output_aliases=aliases,
        compiler_params=pltpu.CompilerParams(vmem_limit_bytes=INPUT_VMEM),
        name="input_grads",
    )(*operands)


def send(value, pairs):
    return lax.ppermute(value, AXES, pairs)


def exchange(arrays, pairs):
    parts = [sum(a[k].astype(F32) for a in arrays) for k in range(4)]
    return [parts[0]] + [send(parts[k].astype(BF), pairs[k]) for k in (1, 2, 3)]


def local(normed, queries, keys, values, attn_grad, kv_proj):
    length, width = normed.shape
    c = lax.axis_index("c")
    place = jnp.stack([c, lax.axis_index("y"), lax.axis_index("zh")]).astype(jnp.int32)
    tokens = length * lax.axis_size(AXES)
    cosine, sine_tab = rope_tables(length, HD)

    half = jnp.where(c == 0, kv_proj[: width // 2], kv_proj[width // 2 :])
    normed_other = send(normed, PARTNER)
    near = [send(half, ALONG_Y[k]) for k in (1, 2, 3)]
    query_grad, kv, away = attention(queries, keys, values, attn_grad, cosine, sine_tab)
    kv_other = send(away, PARTNER)
    across = send(half, Z_HALF)
    scale = tokens ** (-0.5)
    odd = weight_terms(normed, normed_other, kv, kv_other, scale, 1)
    first1 = send(odd[0], FIRST[1])
    first3 = send(odd[1], FIRST[3])
    even = weight_terms(normed, normed_other, kv, kv_other, scale, 0)
    first2 = send(even[1], FIRST[2])
    got = [even[0], first1, first2, first3]

    far = [send(across, ALONG_Y[k]) for k in (1, 2, 3)]
    mine = near + [across] + far
    theirs = [send(block, PARTNER) for block in mine[:4]]
    theirs += [send(block, PARTNER) for block in mine[4:]]
    input_grad = input_grads(place, kv, kv_proj, mine, 0)
    input_grad = input_grads(place, kv, kv_proj, theirs, 1, input_grad)

    got = exchange(got, SECOND)
    got = exchange(got, ALONG_Y)
    total = sum(g.astype(F32) for g in got)
    part, other = total[0], send(total[1], PARTNER)
    weight_grad = jnp.where(
        c == 0, jnp.concatenate([part, other], axis=1), jnp.concatenate([other, part], axis=1)
    )
    return (query_grad, input_grad, weight_grad)


def solution(mesh):
    mesh = Mesh(mesh.devices.reshape(2, 4, 2, 4, 2), AXES)
    spec = P(AXES, None)
    return jax.shard_map(
        local,
        mesh=mesh,
        in_specs=(spec, spec, spec, spec, spec, P(None, ("y", "zh"))),
        out_specs=(spec, spec, spec),
        check_vma=False,
    )
```

time: 259 us -> 128 us (0.49)
  matrix products: 102 us -> 0 us
  waiting for transfers between devices: 118 us -> 24.8 us
  starting transfers between devices: 6.21 us -> 51.1 us
  Pallas kernels: 0 us -> 38.4 us
  between operations: 15.6 us -> 0.84 us
  local copies, waits for them, and re-layouts: 13.9 us -> 6.04 us
  other arithmetic: 2.62 us -> 5.44 us
    dot_general x6 -> x0, matrix products: 91.6 us -> none  [the longest x1 27.4 us: sequence_grads(): jnp.einsum('kgts,skd->tkgd', grad_score, key_heads, preferred_element_typ...]
    all_gather x1 -> x0, waiting for transfers between devices: 73.6 us -> none  [local(): lax.all_gather(kv_proj, 'node', axis=1, tiled=True)]
    ppermute x0 -> x26, starting transfers between devices: none -> 51.1 us  [send(): return lax.ppermute(value, AXES, pairs)]
    reduce_scatter x1 -> x0, waiting for transfers between devices: 44 us -> none  [local(): lax.psum_scatter(local_term.astype(jnp.bfloat16), 'wide', scatter_dimensi...]
    pallas_call x0 -> x5, Pallas kernels: none -> 38.4 us  [the longest x1 14.9 us: attention(): pl.pallas_call(functools.partial(attention_kernel, block=128), in_specs=[...]
    ppermute x0 -> x26, waiting for transfers between devices: none -> 24.8 us  [send(): return lax.ppermute(value, AXES, pairs)]
    sub x1 -> x0, matrix products: 10.2 us -> none  [sequence_grads(): exponent = jnp.exp(scores - row_max)]
    reshape x5 -> x0, local copies, waits for them, and re-layouts: 9.44 us -> none  [the longest x1 3.93 us: sequence_grads(): query_heads = queries.reshape(length, KVH, HQ // KVH, HD)]
  transfers between devices with their start and end apart: 3 -> 26, of which waited for: 2 -> 5; matrix products, arithmetic and copies ran while one was open for 16% -> 4% of each run, Pallas kernels for 0% -> 25%
where the time goes in v1:
time: 128 us; the launch traced here: 127 us
  starting transfers between devices  51.1 us (40%)
  Pallas kernels  38.4 us (30%)
  waiting for transfers between devices  24.8 us (19%)
  local copies, waits for them, and re-layouts  6.04 us (5%)
  other arithmetic  5.44 us (4%)
    ppermute x26, starting transfers between devices, send(): return lax.ppermute(value, AXES, pairs)  51.1 us
    ppermute x26, waiting for transfers between devices, send(): return lax.ppermute(value, AXES, pairs)  24.8 us
    pallas_call x1, Pallas kernels, attention(): pl.pallas_call(functools.partial(attention_kernel, block=128), in_specs=[...  14.9 us
    pallas_call x2, Pallas kernels, weight_terms(): pl.pallas_call(functools.partial(weight_kernel, scale=scale, low=low), in...  13 us
    pallas_call x2, Pallas kernels, input_grads(): pl.pallas_call(input_kernel, grid_spec=pltpu.PrefetchScalarGridSpec(num_s...  10.5 us
    unnamed x32, local copies, waits for them, and re-layouts  6.03 us
    add x2, other arithmetic, exchange(): parts = [sum((a[k].astype(F32) for a in arrays)) for k in range(4)]  3.59 us
  transfers between devices with their start and end apart: 26, of which 5 were waited for; matrix products, arithmetic and copies ran while one was open for 4% of the time, Pallas kernels for 25%

profile of v1, /device:TPU:6, one launch (start us, length us, event | category | flops | bytes accessed | tf_op | source)
XLA Modules:
  0.0 126.6 jit_solution(950509272660689413)
XLA Ops:
  0.7 14.9 %attention.1 = (bf16[512,2048]{1,0:T(8,128)(2,1)}, bf16[2,512,512]{2,1,0:T(8,128)(2,1)}, bf16[512,512]{1,0:T(8,128)(2,1)}) custom-call(bf16[512,2048]{1,0:T(8,128)(2,1)} %q_any.1, bf16[512,512]{1,0:T(8,128)(2,1)} %k_any.1, bf16[512,512]{1,0:T(8,128)(2,1)} %v_any.1, bf16[512,2048]{1,0:T(8,128)(2,1)} %do_any.1, f32[512,64]{1,0:T(8,128)} %constant.17.clone.cos_any, ...), custom_call_target="tpu_custom_call" | custom-call | tf_op jit(solution)/shard_map/attention/pallas_call | solution.py:175
  16.2 1.7 %collective-permute-done.15.kv_other_ref = bf16[512,512]{1,0:T(8,128)(2,1)S(1)} collective-permute-done((bf16[512,512]{1,0:T(8,128)(2,1)}, bf16[512,512]{1,0:T(8,128)(2,1)S(1)}, u32[]{:S(2)}, u32[]{:S(2)}) %collective-permute-start.15) | collective-permute-done | bytes 524320 | tf_op jit(solution)/shard_map/ppermute | solution.py:342
  18.8 6.5 %weight_terms.3 = (bf16[4,4,2,32,512]{4,3,2,1,0:T(8,128)(2,1)}, bf16[4,4,2,32,512]{4,3,2,1,0:T(8,128)(2,1)}) custom-call(bf16[512,4096]{1,0:T(8,128)(2,1)} %own_ref.3, bf16[512,4096]{1,0:T(8,128)(2,1)} %collective-permute-done.14.other_ref, bf16[2,512,512]{2,1,0:T(8,128)(2,1)} %get-tuple-element.11.refs_0_.refs_1_.refs_2_.refs_3_.refs_4_.refs_5_.refs_6_.refs_7_.kv_ref, ...), custom_call_target="tpu_custom_call" | custom-call | tf_op jit(solution)/shard_map/weight_terms/pallas_call | solution.py:269
  25.3 0.8 collective-permute-start.16
  26.2 6.5 %weight_terms.2 = (bf16[4,4,2,32,512]{4,3,2,1,0:T(8,128)(2,1)}, bf16[4,4,2,32,512]{4,3,2,1,0:T(8,128)(2,1)}) custom-call(bf16[512,4096]{1,0:T(8,128)(2,1)} %own_ref.3, bf16[512,4096]{1,0:T(8,128)(2,1)} %collective-permute-done.14.other_ref, bf16[2,512,512]{2,1,0:T(8,128)(2,1)} %get-tuple-element.11.refs_0_.refs_1_.refs_2_.refs_3_.refs_4_.refs_5_.refs_6_.refs_7_.kv_ref, ...), custom_call_target="tpu_custom_call" | custom-call | tf_op jit(solution)/shard_map/weight_terms/pallas_call | solution.py:269
  32.6 1.1 collective-permute-start.17
  33.8 2.9 %collective-permute-start.18 = (bf16[4,4,2,32,512]{4,3,2,1,0:T(8,128)(2,1)}, bf16[4,4,2,32,512]{4,3,2,1,0:T(8,128)(2,1)}, u32[]{:S(2)}, u32[]{:S(2)}) collective-permute-start(bf16[4,4,2,32,512]{4,3,2,1,0:T(8,128)(2,1)} %get-tuple-element.16), channel_id=1, source_target_pairs={{0,48},{1,49},{2,50},{3,51},{4,52},{5,53},{6,54},{7,55},{8,73},{9,... | collective-permute-start | bytes 3145736 | tf_op jit(solution)/shard_map/ppermute | solution.py:342
  36.8 4.0 %collective-permute-start.6 = (bf16[2048,128]{1,0:T(8,128)(2,1)S(1)}, bf16[2048,128]{1,0:T(8,128)(2,1)S(1)}, u32[]{:S(2)}, u32[]{:S(2)}) collective-permute-start(bf16[2048,128]{1,0:T(8,128)(2,1)S(1)} %slice_select_fusion), channel_id=1, source_target_pairs={{0,1},{1,0},{2,3},{3,2},{4,5},{5,4},{6,7},{7,6},{8,9},{9,8},{10,11... | collective-permute-start | bytes 1572872 | tf_op jit(solution)/shard_map/ppermute | solution.py:342
  40.8 1.6 %collective-permute-start = (bf16[2048,128]{1,0:T(8,128)(2,1)S(1)}, bf16[2048,128]{1,0:T(8,128)(2,1)S(1)}, u32[]{:S(2)}, u32[]{:S(2)}) collective-permute-start(bf16[2048,128]{1,0:T(8,128)(2,1)S(1)} %slice_select_fusion), channel_id=1, source_target_pairs={{0,2},{1,3},{2,0},{3,1},{4,6},{5,7},{6,4},{7,5},{8,10},{9,11},{10,... | collective-permute-start | bytes 1572872 | tf_op jit(solution)/shard_map/ppermute | solution.py:342
  42.4 2.9 %collective-permute-start.2 = (bf16[2048,128]{1,0:T(8,128)(2,1)S(1)}, bf16[2048,128]{1,0:T(8,128)(2,1)}, u32[]{:S(2)}, u32[]{:S(2)}) collective-permute-start(bf16[2048,128]{1,0:T(8,128)(2,1)S(1)} %slice_select_fusion), channel_id=1, source_target_pairs={{0,4},{1,5},{2,6},{3,7},{4,0},{5,1},{6,2},{7,3},{8,12},{9,13},{10,... | collective-permute-start | bytes 1572872 | tf_op jit(solution)/shard_map/ppermute | solution.py:342
  45.3 6.4 %collective-permute-done.17 = bf16[4,4,2,32,512]{4,3,2,1,0:T(8,128)(2,1)} collective-permute-done((bf16[4,4,2,32,512]{4,3,2,1,0:T(8,128)(2,1)}, bf16[4,4,2,32,512]{4,3,2,1,0:T(8,128)(2,1)}, u32[]{:S(2)}, u32[]{:S(2)}) %collective-permute-start.17) | collective-permute-done | bytes 1048608 | tf_op jit(solution)/shard_map/ppermute | solution.py:342
  51.6 3.1 %collective-permute-start.4 = (bf16[2048,128]{1,0:T(8,128)(2,1)S(1)}, bf16[2048,128]{1,0:T(8,128)(2,1)S(1)}, u32[]{:S(2)}, u32[]{:S(2)}) collective-permute-start(bf16[2048,128]{1,0:T(8,128)(2,1)S(1)} %slice_select_fusion), channel_id=1, source_target_pairs={{0,6},{1,7},{2,4},{3,5},{4,2},{5,3},{6,0},{7,1},{8,14},{9,15},{10,... | collective-permute-start | bytes 1572872 | tf_op jit(solution)/shard_map/ppermute | solution.py:342
  54.8 6.6 %collective-permute-done.18 = bf16[4,4,2,32,512]{4,3,2,1,0:T(8,128)(2,1)} collective-permute-done((bf16[4,4,2,32,512]{4,3,2,1,0:T(8,128)(2,1)}, bf16[4,4,2,32,512]{4,3,2,1,0:T(8,128)(2,1)}, u32[]{:S(2)}, u32[]{:S(2)}) %collective-permute-start.18) | collective-permute-done | bytes 1048608 | tf_op jit(solution)/shard_map/ppermute | solution.py:342
  61.3 2.8 %fusion = (bf16[4,2,32,512]{3,2,1,0:T(8,128)(2,1)S(1)}, bf16[4,2,32,512]{3,2,1,0:T(8,128)(2,1)S(1)}, bf16[4,2,32,512]{3,2,1,0:T(8,128)(2,1)S(1)}, f32[1,4,2,32,512]{4,3,2,1,0:T(8,128)S(1)}) fusion(bf16[4,4,2,32,512]{4,3,2,1,0:T(8,128)(2,1)} %collective-permute-done.18, bf16[4,4,2,32,512]{4,3,2,1,0:T(8,128)(2,1)} %collective-permute-done.17, ...), kind=kLoop, calls=%fused_computation.5 | loop fusion | flops 4063232 | bytes 5505024 | tf_op jit(solution)/shard_map/add | solution.py:346
  64.2 2.2 %collective-permute-start.19 = (bf16[4,2,32,512]{3,2,1,0:T(8,128)(2,1)S(1)}, bf16[4,2,32,512]{3,2,1,0:T(8,128)(2,1)S(1)}, u32[]{:S(2)}, u32[]{:S(2)}) collective-permute-start(bf16[4,2,32,512]{3,2,1,0:T(8,128)(2,1)S(1)} %get-tuple-element.17), channel_id=1, source_target_pairs={{0,64},{1,65},{2,66},{3,67},{4,68},{5,69},{6,70},{7,71},{8,24},{9,... | collective-permute-start | bytes 786440 | tf_op jit(solution)/shard_map/ppermute | solution.py:342
  66.4 3.6 %collective-permute-start.20 = (bf16[4,2,32,512]{3,2,1,0:T(8,128)(2,1)S(1)}, bf16[4,2,32,512]{3,2,1,0:T(8,128)(2,1)S(1)}, u32[]{:S(2)}, u32[]{:S(2)}) collective-permute-start(bf16[4,2,32,512]{3,2,1,0:T(8,128)(2,1)S(1)} %get-tuple-element.19), channel_id=1, source_target_pairs={{0,1},{1,0},{2,3},{3,2},{4,5},{5,4},{6,7},{7,6},{8,40},{9,41},{10,... | collective-permute-start | bytes 786440 | tf_op jit(solution)/shard_map/ppermute | solution.py:342
  70.0 3.5 %collective-permute-start.10 = (bf16[2048,128]{1,0:T(8,128)(2,1)S(1)}, bf16[2048,128]{1,0:T(8,128)(2,1)S(1)}, u32[]{:S(2)}, u32[]{:S(2)}) collective-permute-start(bf16[2048,128]{1,0:T(8,128)(2,1)S(1)} %collective-permute-done.6.refs_12_), channel_id=1, source_target_pairs={{0,4},{1,5},{2,6},{3,7},{4,0},{5,1},{6,2},{7,3},{8,12},{9,13},{10,... | collective-permute-start | bytes 1572872 | tf_op jit(solution)/shard_map/ppermute | solution.py:342
  73.5 8.0 %collective-permute-done.4.refs_11_ = bf16[2048,128]{1,0:T(8,128)(2,1)S(1)} collective-permute-done((bf16[2048,128]{1,0:T(8,128)(2,1)S(1)}, bf16[2048,128]{1,0:T(8,128)(2,1)S(1)}, u32[]{:S(2)}, u32[]{:S(2)}) %collective-permute-start.4) | collective-permute-done | bytes 524320 | tf_op jit(solution)/shard_map/ppermute | solution.py:342
  81.6 8.1 %collective-permute-start.7 = (bf16[2048,128]{1,0:T(8,128)(2,1)S(1)}, bf16[2048,128]{1,0:T(8,128)(2,1)S(1)}, u32[]{:S(2)}, u32[]{:S(2)}) collective-permute-start(bf16[2048,128]{1,0:T(8,128)(2,1)S(1)} %collective-permute-done.6.refs_12_), channel_id=1, source_target_pairs={{0,8},{1,9},{2,10},{3,11},{4,12},{5,13},{6,14},{7,15},{8,0},{9,1},... | collective-permute-start | bytes 1572872 | tf_op jit(solution)/shard_map/ppermute | solution.py:342
  89.7 2.8 %collective-permute-start.1 = (bf16[2048,128]{1,0:T(8,128)(2,1)S(1)}, bf16[2048,128]{1,0:T(8,128)(2,1)}, u32[]{:S(2)}, u32[]{:S(2)}) collective-permute-start(bf16[2048,128]{1,0:T(8,128)(2,1)S(1)} %collective-permute-done.refs_9_), channel_id=1, source_target_pairs={{0,8},{1,9},{2,10},{3,11},{4,12},{5,13},{6,14},{7,15},{8,0},{9,1},... | collective-permute-start | bytes 1572872 | tf_op jit(solution)/shard_map/ppermute | solution.py:342
  93.3 1.3 %collective-permute-start.22 = (bf16[2,32,512]{2,1,0:T(8,128)(2,1)}, bf16[2,32,512]{2,1,0:T(8,128)(2,1)S(1)}, u32[]{:S(2)}, u32[]{:S(2)}) collective-permute-start(bf16[2,32,512]{2,1,0:T(8,128)(2,1)} %get-tuple-element.21), channel_id=1, source_target_pairs={{0,2},{1,3},{2,0},{3,1},{4,6},{5,7},{6,4},{7,5},{8,10},{9,11},{10,... | collective-permute-start | bytes 196616 | tf_op jit(solution)/shard_map/ppermute | solution.py:342
  94.5 2.0 %collective-permute-done.12.refs_15_ = bf16[2048,128]{1,0:T(8,128)(2,1)S(1)} collective-permute-done((bf16[2048,128]{1,0:T(8,128)(2,1)S(1)}, bf16[2048,128]{1,0:T(8,128)(2,1)S(1)}, u32[]{:S(2)}, u32[]{:S(2)}) %collective-permute-start.12) | collective-permute-done | bytes 524320 | tf_op jit(solution)/shard_map/ppermute | solution.py:342
  96.5 0.9 collective-permute-start.23
  99.0 8.0 %collective-permute-start.3 = (bf16[2048,128]{1,0:T(8,128)(2,1)}, bf16[2048,128]{1,0:T(8,128)(2,1)}, u32[]{:S(2)}, u32[]{:S(2)}) collective-permute-start(bf16[2048,128]{1,0:T(8,128)(2,1)} %collective-permute-done.2.refs_10_), channel_id=1, source_target_pairs={{0,8},{1,9},{2,10},{3,11},{4,12},{5,13},{6,14},{7,15},{8,0},{9,1},... | collective-permute-start | bytes 1572872 | tf_op jit(solution)/shard_map/ppermute | solution.py:342
  107.5 1.9 %collective-permute-start.13 = (bf16[2048,128]{1,0:T(8,128)(2,1)}, bf16[2048,128]{1,0:T(8,128)(2,1)S(1)}, u32[]{:S(2)}, u32[]{:S(2)}) collective-permute-start(bf16[2048,128]{1,0:T(8,128)(2,1)} %copy-done.6), channel_id=1, source_target_pairs={{0,8},{1,9},{2,10},{3,11},{4,12},{5,13},{6,14},{7,15},{8,0},{9,1},... | collective-permute-start | bytes 1572872 | tf_op jit(solution)/shard_map/ppermute | solution.py:342
  109.6 1.1 fusion.21
  111.2 1.0 copy-done.3
  112.2 1.0 copy-done.5
  113.3 1.0 copy-done.7
  114.3 1.0 copy-done.9
  115.3 5.2 %input_grads.2.refs_16_ = bf16[512,4096]{1,0:T(8,128)(2,1)} custom-call(s32[3]{0:T(128)S(1)} %pad_add_fusion.place, bf16[2,512,512]{2,1,0:T(8,128)(2,1)S(1)} %copy-done, bf16[2,512,512]{2,1,0:T(8,128)(2,1)S(1)} %copy-done, bf16[2,512,512]{2,1,0:T(8,128)(2,1)S(1)} %copy-done, bf16[2,512,512]{2,1,0:T(8,128)(2,1)S(1)} %copy-done, ...), custom_call_target="tpu_custom_call" | custom-call | tf_op jit(solution)/shard_map/input_grads/pallas_call | solution.py:326
  120.6 5.3 %input_grads.3 = bf16[512,4096]{1,0:T(8,128)(2,1)} custom-call(s32[3]{0:T(128)S(1)} %pad_add_fusion.place, bf16[2,512,512]{2,1,0:T(8,128)(2,1)S(1)} %copy-done, bf16[2,512,512]{2,1,0:T(8,128)(2,1)S(1)} %copy-done, bf16[2,512,512]{2,1,0:T(8,128)(2,1)S(1)} %copy-done, bf16[2,512,512]{2,1,0:T(8,128)(2,1)S(1)} %copy-done, ...), custom_call_target="tpu_custom_call", output_to_operand_aliasing={{}: (17, {})} | custom-call | tf_op jit(solution)/shard_map/input_grads/pallas_call | solution.py:326
  (64 shorter events, 5.9 us)
Async XLA Ops:
  0.6 17.4 %collective-permute-start.14 = (bf16[512,4096]{1,0:T(8,128)(2,1)}, bf16[512,4096]{1,0:T(8,128)(2,1)}, u32[]{:S(2)}, u32[]{:S(2)}) collective-permute-start(bf16[512,4096]{1,0:T(8,128)(2,1)} %own_ref.3), channel_id=1, source_target_pairs={{0,8},{1,9},{2,10},{3,11},{4,12},{5,13},{6,14},{7,15},{8,0},{9,1},... | collective-permute-start | bytes 12582920 | tf_op jit(solution)/shard_map/ppermute | solution.py:342
  15.7 2.3 %collective-permute-start.15 = (bf16[512,512]{1,0:T(8,128)(2,1)}, bf16[512,512]{1,0:T(8,128)(2,1)S(1)}, u32[]{:S(2)}, u32[]{:S(2)}) collective-permute-start(bf16[512,512]{1,0:T(8,128)(2,1)} %get-tuple-element.12), channel_id=1, source_target_pairs={{0,8},{1,9},{2,10},{3,11},{4,12},{5,13},{6,14},{7,15},{8,0},{9,1},... | collective-permute-start | bytes 1572872 | tf_op jit(solution)/shard_map/ppermute | solution.py:342
  25.3 11.4 %copy-start.1 = (bf16[4096,128]{1,0:T(8,128)(2,1)S(1)}, bf16[4096,128]{1,0:T(8,128)(2,1)}, u32[]{:S(2)}) copy-start(bf16[4096,128]{1,0:T(8,128)(2,1)} %refs_8_.3) | copy-start | bytes 3145732
  25.3 17.0 %collective-permute-start.16 = (bf16[4,4,2,32,512]{4,3,2,1,0:T(8,128)(2,1)}, bf16[4,4,2,32,512]{4,3,2,1,0:T(8,128)(2,1)}, u32[]{:S(2)}, u32[]{:S(2)}) collective-permute-start(bf16[4,4,2,32,512]{4,3,2,1,0:T(8,128)(2,1)} %get-tuple-element.14), channel_id=1, source_target_pairs={{0,16},{1,17},{2,18},{3,19},{4,20},{5,21},{6,22},{7,23},{8,72},{9,... | collective-permute-start | bytes 3145736 | tf_op jit(solution)/shard_map/ppermute | solution.py:342
  32.6 19.0 %collective-permute-start.17 = (bf16[4,4,2,32,512]{4,3,2,1,0:T(8,128)(2,1)}, bf16[4,4,2,32,512]{4,3,2,1,0:T(8,128)(2,1)}, u32[]{:S(2)}, u32[]{:S(2)}) collective-permute-start(bf16[4,4,2,32,512]{4,3,2,1,0:T(8,128)(2,1)} %get-tuple-element.15), channel_id=1, source_target_pairs={{0,32},{1,33},{2,34},{3,35},{4,36},{5,37},{6,38},{7,39},{8,9},{9,8... | collective-permute-start | bytes 3145736 | tf_op jit(solution)/shard_map/ppermute | solution.py:342
  33.8 27.6 %collective-permute-start.18 = (bf16[4,4,2,32,512]{4,3,2,1,0:T(8,128)(2,1)}, bf16[4,4,2,32,512]{4,3,2,1,0:T(8,128)(2,1)}, u32[]{:S(2)}, u32[]{:S(2)}) collective-permute-start(bf16[4,4,2,32,512]{4,3,2,1,0:T(8,128)(2,1)} %get-tuple-element.16), channel_id=1, source_target_pairs={{0,48},{1,49},{2,50},{3,51},{4,52},{5,53},{6,54},{7,55},{8,73},{9,... | collective-permute-start | bytes 3145736 | tf_op jit(solution)/shard_map/ppermute | solution.py:342
  36.8 74.4 %copy-start = (bf16[2,512,512]{2,1,0:T(8,128)(2,1)S(1)}, bf16[2,512,512]{2,1,0:T(8,128)(2,1)}, u32[]{:S(2)}) copy-start(bf16[2,512,512]{2,1,0:T(8,128)(2,1)} %get-tuple-element.11.refs_0_.refs_1_.refs_2_.refs_3_.refs_4_.refs_5_.refs_6_.refs_7_.kv_ref) | copy-start | bytes 3145732
  36.8 29.6 %collective-permute-start.6 = (bf16[2048,128]{1,0:T(8,128)(2,1)S(1)}, bf16[2048,128]{1,0:T(8,128)(2,1)S(1)}, u32[]{:S(2)}, u32[]{:S(2)}) collective-permute-start(bf16[2048,128]{1,0:T(8,128)(2,1)S(1)} %slice_select_fusion), channel_id=1, source_target_pairs={{0,1},{1,0},{2,3},{3,2},{4,5},{5,4},{6,7},{7,6},{8,9},{9,8},{10,11... | collective-permute-start | bytes 1572872 | tf_op jit(solution)/shard_map/ppermute | solution.py:342
  40.8 29.2 %collective-permute-start = (bf16[2048,128]{1,0:T(8,128)(2,1)S(1)}, bf16[2048,128]{1,0:T(8,128)(2,1)S(1)}, u32[]{:S(2)}, u32[]{:S(2)}) collective-permute-start(bf16[2048,128]{1,0:T(8,128)(2,1)S(1)} %slice_select_fusion), channel_id=1, source_target_pairs={{0,2},{1,3},{2,0},{3,1},{4,6},{5,7},{6,4},{7,5},{8,10},{9,11},{10,... | collective-permute-start | bytes 1572872 | tf_op jit(solution)/shard_map/ppermute | solution.py:342
  42.4 27.6 %collective-permute-start.2 = (bf16[2048,128]{1,0:T(8,128)(2,1)S(1)}, bf16[2048,128]{1,0:T(8,128)(2,1)}, u32[]{:S(2)}, u32[]{:S(2)}) collective-permute-start(bf16[2048,128]{1,0:T(8,128)(2,1)S(1)} %slice_select_fusion), channel_id=1, source_target_pairs={{0,4},{1,5},{2,6},{3,7},{4,0},{5,1},{6,2},{7,3},{8,12},{9,13},{10,... | collective-permute-start | bytes 1572872 | tf_op jit(solution)/shard_map/ppermute | solution.py:342
  51.6 29.9 %collective-permute-start.4 = (bf16[2048,128]{1,0:T(8,128)(2,1)S(1)}, bf16[2048,128]{1,0:T(8,128)(2,1)S(1)}, u32[]{:S(2)}, u32[]{:S(2)}) collective-permute-start(bf16[2048,128]{1,0:T(8,128)(2,1)S(1)} %slice_select_fusion), channel_id=1, source_target_pairs={{0,6},{1,7},{2,4},{3,5},{4,2},{5,3},{6,0},{7,1},{8,14},{9,15},{10,... | collective-permute-start | bytes 1572872 | tf_op jit(solution)/shard_map/ppermute | solution.py:342
  64.2 33.8 %copy-start.13 = (f32[1,4,2,32,512]{4,3,2,1,0:T(8,128)}, f32[1,4,2,32,512]{4,3,2,1,0:T(8,128)S(1)}, u32[]{:S(2)}) copy-start(f32[1,4,2,32,512]{4,3,2,1,0:T(8,128)S(1)} %get-tuple-element.20) | copy-start | bytes 1572868
  64.2 17.3 %collective-permute-start.19 = (bf16[4,2,32,512]{3,2,1,0:T(8,128)(2,1)S(1)}, bf16[4,2,32,512]{3,2,1,0:T(8,128)(2,1)S(1)}, u32[]{:S(2)}, u32[]{:S(2)}) collective-permute-start(bf16[4,2,32,512]{3,2,1,0:T(8,128)(2,1)S(1)} %get-tuple-element.17), channel_id=1, source_target_pairs={{0,64},{1,65},{2,66},{3,67},{4,68},{5,69},{6,70},{7,71},{8,24},{9,... | collective-permute-start | bytes 786440 | tf_op jit(solution)/shard_map/ppermute | solution.py:342
  66.4 15.2 %collective-permute-start.20 = (bf16[4,2,32,512]{3,2,1,0:T(8,128)(2,1)S(1)}, bf16[4,2,32,512]{3,2,1,0:T(8,128)(2,1)S(1)}, u32[]{:S(2)}, u32[]{:S(2)}) collective-permute-start(bf16[4,2,32,512]{3,2,1,0:T(8,128)(2,1)S(1)} %get-tuple-element.19), channel_id=1, source_target_pairs={{0,1},{1,0},{2,3},{3,2},{4,5},{5,4},{6,7},{7,6},{8,40},{9,41},{10,... | collective-permute-start | bytes 786440 | tf_op jit(solution)/shard_map/ppermute | solution.py:342
  70.0 19.7 %collective-permute-start.21 = (bf16[4,2,32,512]{3,2,1,0:T(8,128)(2,1)S(1)}, bf16[4,2,32,512]{3,2,1,0:T(8,128)(2,1)S(1)}, u32[]{:S(2)}, u32[]{:S(2)}) collective-permute-start(bf16[4,2,32,512]{3,2,1,0:T(8,128)(2,1)S(1)} %get-tuple-element.18), channel_id=1, source_target_pairs={{0,65},{1,64},{2,67},{3,66},{4,69},{5,68},{6,71},{7,70},{8,56},{9,... | collective-permute-start | bytes 786440 | tf_op jit(solution)/shard_map/ppermute | solution.py:342
  70.0 23.3 %collective-permute-start.10 = (bf16[2048,128]{1,0:T(8,128)(2,1)S(1)}, bf16[2048,128]{1,0:T(8,128)(2,1)S(1)}, u32[]{:S(2)}, u32[]{:S(2)}) collective-permute-start(bf16[2048,128]{1,0:T(8,128)(2,1)S(1)} %collective-permute-done.6.refs_12_), channel_id=1, source_target_pairs={{0,4},{1,5},{2,6},{3,7},{4,0},{5,1},{6,2},{7,3},{8,12},{9,13},{10,... | collective-permute-start | bytes 1572872 | tf_op jit(solution)/shard_map/ppermute | solution.py:342
  81.5 16.5 %copy-start.2 = (bf16[2048,128]{1,0:T(8,128)(2,1)}, bf16[2048,128]{1,0:T(8,128)(2,1)S(1)}, u32[]{:S(2)}) copy-start(bf16[2048,128]{1,0:T(8,128)(2,1)S(1)} %collective-permute-done.4.refs_11_) | copy-start | bytes 1572868
  81.5 15.0 %collective-permute-start.12 = (bf16[2048,128]{1,0:T(8,128)(2,1)S(1)}, bf16[2048,128]{1,0:T(8,128)(2,1)S(1)}, u32[]{:S(2)}, u32[]{:S(2)}) collective-permute-start(bf16[2048,128]{1,0:T(8,128)(2,1)S(1)} %collective-permute-done.6.refs_12_), channel_id=1, source_target_pairs={{0,6},{1,7},{2,4},{3,5},{4,2},{5,3},{6,0},{7,1},{8,14},{9,15},{10,... | collective-permute-start | bytes 1572872 | tf_op jit(solution)/shard_map/ppermute | solution.py:342
  81.5 15.9 %collective-permute-start.8 = (bf16[2048,128]{1,0:T(8,128)(2,1)S(1)}, bf16[2048,128]{1,0:T(8,128)(2,1)S(1)}, u32[]{:S(2)}, u32[]{:S(2)}) collective-permute-start(bf16[2048,128]{1,0:T(8,128)(2,1)S(1)} %collective-permute-done.6.refs_12_), channel_id=1, source_target_pairs={{0,2},{1,3},{2,0},{3,1},{4,6},{5,7},{6,4},{7,5},{8,10},{9,11},{10,... | collective-permute-start | bytes 1572872 | tf_op jit(solution)/shard_map/ppermute | solution.py:342
  81.6 16.4 %copy-start.14 = (bf16[4,2,32,512]{3,2,1,0:T(8,128)(2,1)}, bf16[4,2,32,512]{3,2,1,0:T(8,128)(2,1)S(1)}, u32[]{:S(2)}) copy-start(bf16[4,2,32,512]{3,2,1,0:T(8,128)(2,1)S(1)} %collective-permute-done.20) | copy-start | bytes 786436
  81.6 16.3 %collective-permute-start.7 = (bf16[2048,128]{1,0:T(8,128)(2,1)S(1)}, bf16[2048,128]{1,0:T(8,128)(2,1)S(1)}, u32[]{:S(2)}, u32[]{:S(2)}) collective-permute-start(bf16[2048,128]{1,0:T(8,128)(2,1)S(1)} %collective-permute-done.6.refs_12_), channel_id=1, source_target_pairs={{0,8},{1,9},{2,10},{3,11},{4,12},{5,13},{6,14},{7,15},{8,0},{9,1},... | collective-permute-start | bytes 1572872 | tf_op jit(solution)/shard_map/ppermute | solution.py:342
  89.7 8.3 %copy-start.15 = (bf16[4,2,32,512]{3,2,1,0:T(8,128)(2,1)}, bf16[4,2,32,512]{3,2,1,0:T(8,128)(2,1)S(1)}, u32[]{:S(2)}) copy-start(bf16[4,2,32,512]{3,2,1,0:T(8,128)(2,1)S(1)} %collective-permute-done.21) | copy-start | bytes 786436
  89.7 17.3 %collective-permute-start.1 = (bf16[2048,128]{1,0:T(8,128)(2,1)S(1)}, bf16[2048,128]{1,0:T(8,128)(2,1)}, u32[]{:S(2)}, u32[]{:S(2)}) collective-permute-start(bf16[2048,128]{1,0:T(8,128)(2,1)S(1)} %collective-permute-done.refs_9_), channel_id=1, source_target_pairs={{0,8},{1,9},{2,10},{3,11},{4,12},{5,13},{6,14},{7,15},{8,0},{9,1},... | collective-permute-start | bytes 1572872 | tf_op jit(solution)/shard_map/ppermute | solution.py:342
  93.3 13.8 %collective-permute-start.22 = (bf16[2,32,512]{2,1,0:T(8,128)(2,1)}, bf16[2,32,512]{2,1,0:T(8,128)(2,1)S(1)}, u32[]{:S(2)}, u32[]{:S(2)}) collective-permute-start(bf16[2,32,512]{2,1,0:T(8,128)(2,1)} %get-tuple-element.21), channel_id=1, source_target_pairs={{0,2},{1,3},{2,0},{3,1},{4,6},{5,7},{6,4},{7,5},{8,10},{9,11},{10,... | collective-permute-start | bytes 196616 | tf_op jit(solution)/shard_map/ppermute | solution.py:342
  96.5 11.0 %collective-permute-start.23 = (bf16[2,32,512]{2,1,0:T(8,128)(2,1)}, bf16[2,32,512]{2,1,0:T(8,128)(2,1)}, u32[]{:S(2)}, u32[]{:S(2)}) collective-permute-start(bf16[2,32,512]{2,1,0:T(8,128)(2,1)} %get-tuple-element.23), channel_id=1, source_target_pairs={{0,4},{1,5},{2,6},{3,7},{4,0},{5,1},{6,2},{7,3},{8,12},{9,13},{10,... | collective-permute-start | bytes 196616 | tf_op jit(solution)/shard_map/ppermute | solution.py:342
  97.5 12.0 %collective-permute-start.24 = (bf16[2,32,512]{2,1,0:T(8,128)(2,1)S(1)}, bf16[2,32,512]{2,1,0:T(8,128)(2,1)}, u32[]{:S(2)}, u32[]{:S(2)}) collective-permute-start(bf16[2,32,512]{2,1,0:T(8,128)(2,1)S(1)} %get-tuple-element.22), channel_id=1, source_target_pairs={{0,6},{1,7},{2,4},{3,5},{4,2},{5,3},{6,0},{7,1},{8,14},{9,15},{10,... | collective-permute-start | bytes 196616 | tf_op jit(solution)/shard_map/ppermute | solution.py:342
  99.0 11.6 %collective-permute-start.3 = (bf16[2048,128]{1,0:T(8,128)(2,1)}, bf16[2048,128]{1,0:T(8,128)(2,1)}, u32[]{:S(2)}, u32[]{:S(2)}) collective-permute-start(bf16[2048,128]{1,0:T(8,128)(2,1)} %collective-permute-done.2.refs_10_), channel_id=1, source_target_pairs={{0,8},{1,9},{2,10},{3,11},{4,12},{5,13},{6,14},{7,15},{8,0},{9,1},... | collective-permute-start | bytes 1572872 | tf_op jit(solution)/shard_map/ppermute | solution.py:342
  107.0 13.5 %collective-permute-start.5 = (bf16[2048,128]{1,0:T(8,128)(2,1)}, bf16[2048,128]{1,0:T(8,128)(2,1)S(1)}, u32[]{:S(2)}, u32[]{:S(2)}) collective-permute-start(bf16[2048,128]{1,0:T(8,128)(2,1)} %copy-done.2), channel_id=1, source_target_pairs={{0,8},{1,9},{2,10},{3,11},{4,12},{5,13},{6,14},{7,15},{8,0},{9,1},... | collective-permute-start | bytes 1572872 | tf_op jit(solution)/shard_map/ppermute | solution.py:342
  107.0 13.5 %collective-permute-start.11 = (bf16[2048,128]{1,0:T(8,128)(2,1)}, bf16[2048,128]{1,0:T(8,128)(2,1)S(1)}, u32[]{:S(2)}, u32[]{:S(2)}) collective-permute-start(bf16[2048,128]{1,0:T(8,128)(2,1)} %copy-done.4), channel_id=1, source_target_pairs={{0,8},{1,9},{2,10},{3,11},{4,12},{5,13},{6,14},{7,15},{8,0},{9,1},... | collective-permute-start | bytes 1572872 | tf_op jit(solution)/shard_map/ppermute | solution.py:342
  107.5 13.0 %collective-permute-start.13 = (bf16[2048,128]{1,0:T(8,128)(2,1)}, bf16[2048,128]{1,0:T(8,128)(2,1)S(1)}, u32[]{:S(2)}, u32[]{:S(2)}) collective-permute-start(bf16[2048,128]{1,0:T(8,128)(2,1)} %copy-done.6), channel_id=1, source_target_pairs={{0,8},{1,9},{2,10},{3,11},{4,12},{5,13},{6,14},{7,15},{8,0},{9,1},... | collective-permute-start | bytes 1572872 | tf_op jit(solution)/shard_map/ppermute | solution.py:342
  109.4 11.1 %collective-permute-start.9 = (bf16[2048,128]{1,0:T(8,128)(2,1)}, bf16[2048,128]{1,0:T(8,128)(2,1)S(1)}, u32[]{:S(2)}, u32[]{:S(2)}) collective-permute-start(bf16[2048,128]{1,0:T(8,128)(2,1)} %copy-done.8), channel_id=1, source_target_pairs={{0,8},{1,9},{2,10},{3,11},{4,12},{5,13},{6,14},{7,15},{8,0},{9,1},... | collective-permute-start | bytes 1572872 | tf_op jit(solution)/shard_map/ppermute | solution.py:342
  110.7 15.2 %collective-permute-start.25 = (f32[32,512]{1,0:T(8,128)S(1)}, f32[32,512]{1,0:T(8,128)S(1)}, u32[]{:S(2)}, u32[]{:S(2)}) collective-permute-start(f32[32,512]{1,0:T(8,128)S(1)} %get-tuple-element.25), channel_id=1, source_target_pairs={{0,8},{1,9},{2,10},{3,11},{4,12},{5,13},{6,14},{7,15},{8,0},{9,1},... | collective-permute-start | bytes 196616 | tf_op jit(solution)/shard_map/ppermute | solution.py:342
  (10 other events, 18.1 us)
